TPU v7x, 32 devices: a whole 2x2x4 slice. The times are simulated.
32 devices in a mesh: seq: 8 (over y, x, core), batch: 4 (over z).
Axes of the slice: x: 2, y: 2, z: 4, core: 2. Of those that a mesh axis runs over, the one named last changes fastest.
Arguments:
- stream_in: bfloat16 [16, 2048, 768], P('batch', 'seq'), may hold values from -6 to 6
- lengths: int32 [16], P('batch'), may hold values from 64 to 2048, as said below
- token_mask: int32 [16, 2048], P('batch', 'seq'), may hold values from 0 to 1, as said below
- norm1_gain: bfloat16 [768], replicated, may hold values from 0.5 to 1.5
- w_qkv: bfloat16 [768, 2304], replicated, may hold values from -0.21875 to 0.21875
- conv_taps: bfloat16 [3, 2304], replicated, may hold values from -3 to 3
- w_out: bfloat16 [768, 768], replicated, may hold values from -1.75 to 1.75
- norm2_gain: bfloat16 [768], replicated, may hold values from 0.5 to 1.5
- w_up: bfloat16 [768, 3072], replicated, may hold values from -0.21875 to 0.21875
- w_down: bfloat16 [3072, 768], replicated, may hold values from -0.109375 to 0.109375
- grad_output: bfloat16 [16, 2048, 768], P('batch', 'seq'), may hold values from -6 to 6
Outputs:
- stream_out: bfloat16 [16, 2048, 768], P('batch', 'seq')
- grad_input: float32 [16, 2048, 768], P('batch', 'seq')
- grad_norm1: float32 [768], P('batch')
- grad_qkv: float32 [768, 2304], P('batch')
- grad_taps: float32 [3, 2304], replicated
- grad_wout: float32 [768, 768], P('batch')
- grad_norm2: float32 [768], P('batch')
- grad_up: float32 [768, 3072], P('batch')
- grad_down: float32 [3072, 768], P('batch')
- block_rms: float32 [3], replicated
Inputs may be any that keep to these rules, and one draw needn't show every extreme that they name: `lengths`: lengths are heavy tailed over 64 to 2048; some sequence has exactly 2048. `token_mask`: 0 or 1; the first position of every sequence is 1.
All inputs are finite; a program needn't handle non-finite values.
Results may differ from a plain program's by a relative error of at most 0.02.
Values may be sent and summed in bfloat16 or wider, within the bound.
A program may use at most 384 MiB of HBM per device.

v0:
```python
import math
import jax
import jax.numpy as jnp
from jax import lax
from jax.sharding import PartitionSpec as P

HEADS = 12
HEAD = 64


def from_behind(value, axis, steps):
    count = lax.axis_size(axis)
    initial, last = (max(0, -steps), min(count, count - steps))
    return lax.ppermute(value, axis, [(source, source + steps) for source in range(initial, last)])


def dense(left_op, right_op):
    return jnp.dot(left_op, right_op, preferred_element_type=jnp.float32)


def norm_forward(values, gain_vec):
    factor = lax.rsqrt(jnp.mean(values * values, axis=-1, keepdims=True) + 1e-06)
    return (values * factor * gain_vec, factor)


def norm_backward(values, factor, gain_vec, upstream):
    weighted = upstream * gain_vec
    inner_mean = jnp.mean(weighted * values, axis=-1, keepdims=True)
    d_values = factor * weighted - values * (factor * factor * factor) * inner_mean
    d_gain = jnp.sum(upstream * values * factor, axis=(0, 1))
    return (d_values, d_gain)


def split_heads(row_block):
    return row_block.reshape(row_block.shape[0], HEADS, HEAD)


def score_block(q_rows, k_rows, q_begin, k_begin, length):
    factor = 1.0 / math.sqrt(HEAD)
    scores = (
        jnp.einsum(
            "qhe,khe->hqk",
            split_heads(q_rows),
            split_heads(k_rows),
            preferred_element_type=jnp.float32,
        )
        * factor
    )
    q_pos = q_begin + jnp.arange(q_rows.shape[0], dtype=jnp.int32)
    k_pos = k_begin + jnp.arange(k_rows.shape[0], dtype=jnp.int32)
    allowed = (k_pos[None, :] <= q_pos[:, None]) & (k_pos[None, :] < length)
    return (scores, allowed[None])


def attend_forward(q_rows, k_rows, v_rows, length, offset):
    scores, allowed = score_block(q_rows, k_rows, offset, 0, length)
    masked = jnp.where(allowed, scores, -1e30)
    row_max = jnp.max(masked, axis=-1, keepdims=True)
    exp_terms = jnp.exp(masked - row_max)
    row_total = jnp.sum(exp_terms, axis=-1, keepdims=True)
    weights = (exp_terms / row_total).astype(jnp.bfloat16)
    attended = jnp.einsum(
        "hqk,khe->qhe", weights, split_heads(v_rows), preferred_element_type=jnp.float32
    )
    return (attended.reshape(q_rows.shape[0], HEADS * HEAD), (row_max + jnp.log(row_total))[..., 0])


def attend_backward(q_rows, k_rows, v_rows, d_rows, log_total, length, offset):
    scores, allowed = score_block(q_rows, k_rows, offset, 0, length)
    prob_rows = jnp.where(allowed, jnp.exp(scores - log_total[..., None]), 0.0)
    d_probs = jnp.einsum(
        "qhe,khe->hqk", split_heads(d_rows), split_heads(v_rows), preferred_element_type=jnp.float32
    )
    delta_rows = jnp.sum(prob_rows * d_probs, axis=-1, keepdims=True)
    d_scores = (prob_rows * (d_probs - delta_rows)).astype(jnp.bfloat16)
    factor = 1.0 / math.sqrt(HEAD)
    d_query = (
        jnp.einsum(
            "hqk,khe->qhe", d_scores, split_heads(k_rows), preferred_element_type=jnp.float32
        ).reshape(q_rows.shape[0], HEADS * HEAD)
        * factor
    )
    return (d_query, d_scores, prob_rows, delta_rows[..., 0])


def shards(
    stream_in,
    lengths,
    token_mask,
    norm1_gain,
    w_qkv,
    conv_taps,
    w_out,
    norm2_gain,
    w_up,
    w_down,
    grad_output,
):
    seq_count, block_len, model_width = stream_in.shape
    offset = lax.axis_index("seq") * block_len
    factor = 1.0 / math.sqrt(HEAD)
    gain_one = norm1_gain.astype(jnp.float32)
    gain_two = norm2_gain.astype(jnp.float32)
    taps = conv_taps.astype(jnp.float32)
    resid = stream_in.astype(jnp.float32)
    positions = offset + jnp.arange(block_len, dtype=jnp.int32)
    stat_weight = token_mask.astype(jnp.float32) * (positions[None, :] < lengths[:, None]).astype(
        jnp.float32
    )
    cotangent = (grad_output.astype(jnp.float32) * stat_weight[..., None]).astype(jnp.bfloat16)
    normed1, factor_one = norm_forward(resid, gain_one)
    normed1_low = normed1.astype(jnp.bfloat16)
    projected = dense(normed1_low, w_qkv)
    rim_rows = from_behind(projected[:, block_len - 2 :], "seq", 1)
    extended = jnp.concatenate([rim_rows, projected], axis=1)
    mixed = (
        taps[0] * extended[:, 2:]
        + taps[1] * extended[:, 1 : block_len + 1]
        + taps[2] * extended[:, :block_len]
    ).astype(jnp.bfloat16)
    query = mixed[..., :model_width]
    keys_own = mixed[..., model_width : 2 * model_width]
    values_own = mixed[..., 2 * model_width :]
    keys_all, values_all = (
        lax.all_gather(keys_own, "seq", axis=1, tiled=True),
        lax.all_gather(values_own, "seq", axis=1, tiled=True),
    )

    def forward_one(item):
        return attend_forward(item[0], item[1], item[2], item[3], offset)

    attended, log_totals = lax.map(forward_one, (query, keys_all, values_all, lengths))
    attended_low = attended.astype(jnp.bfloat16)
    branch_attn = dense(attended_low, w_out)
    hidden1 = resid + branch_attn
    normed2, factor_two = norm_forward(hidden1, gain_two)
    normed2_low = normed2.astype(jnp.bfloat16)
    up_proj = dense(normed2_low, w_up)
    active = jax.nn.relu(up_proj)
    squared = (active * active).astype(jnp.bfloat16)
    branch_ff = dense(squared, w_down)
    stream_full = hidden1 + branch_ff
    stream_out = stream_full.astype(jnp.bfloat16)

    def masked_square(values):
        return jnp.sum(stat_weight * jnp.sum(values * values, axis=-1))

    local_stats = jnp.stack(
        [
            masked_square(stream_full),
            masked_square(branch_attn),
            masked_square(branch_ff),
            jnp.sum(stat_weight),
        ]
    )
    grad_down = jnp.einsum("scf,scd->fd", squared, cotangent, preferred_element_type=jnp.float32)
    d_squared = jnp.einsum("scd,fd->scf", cotangent, w_down, preferred_element_type=jnp.float32)
    d_up = (2.0 * active * d_squared).astype(jnp.bfloat16)
    grad_up = jnp.einsum("scd,scf->df", normed2_low, d_up, preferred_element_type=jnp.float32)
    d_normed2 = jnp.einsum("scf,df->scd", d_up, w_up, preferred_element_type=jnp.float32)
    d_hidden_norm, grad_norm2 = norm_backward(hidden1, factor_two, gain_two, d_normed2)
    d_hidden1 = cotangent.astype(jnp.float32) + d_hidden_norm
    d_attn = d_hidden1.astype(jnp.bfloat16)
    grad_wout = jnp.einsum("scd,sce->de", attended_low, d_attn, preferred_element_type=jnp.float32)
    d_attended = jnp.einsum(
        "sce,de->scd", d_attn, w_out, preferred_element_type=jnp.float32
    ).astype(jnp.bfloat16)

    def backward_local(item):
        d_query, d_scores, prob_rows, delta_rows = attend_backward(
            item[0], item[1], item[2], item[3], item[4], item[5], offset
        )
        return (d_query, delta_rows)

    d_query_all, delta_all = lax.map(
        backward_local, (query, keys_all, values_all, d_attended, log_totals, lengths)
    )
    lse_rows, delta_rows_all = (
        lax.all_gather(log_totals, "seq", axis=2, tiled=True),
        lax.all_gather(delta_all, "seq", axis=2, tiled=True),
    )
    begin_row = jnp.int32(0)
    q_piece = lax.all_gather(query, "seq", axis=1, tiled=True)
    d_piece = lax.all_gather(d_attended, "seq", axis=1, tiled=True)

    def per_sequence(q_rows, d_rows, k_rows, v_rows, lse_seq, delta_seq, length):
        scores, allowed = score_block(q_rows, k_rows, begin_row, offset, length)
        prob_rows = jnp.where(allowed, jnp.exp(scores - lse_seq[..., None]), 0.0)
        d_probs = jnp.einsum(
            "qhe,khe->hqk",
            split_heads(d_rows),
            split_heads(v_rows),
            preferred_element_type=jnp.float32,
        )
        d_scores = (prob_rows * (d_probs - delta_seq[..., None])).astype(jnp.bfloat16)
        d_keys_part = (
            jnp.einsum(
                "hqk,qhe->khe", d_scores, split_heads(q_rows), preferred_element_type=jnp.float32
            ).reshape(k_rows.shape[0], model_width)
            * factor
        )
        d_values_part = jnp.einsum(
            "hqk,qhe->khe",
            prob_rows.astype(jnp.bfloat16),
            split_heads(d_rows),
            preferred_element_type=jnp.float32,
        ).reshape(k_rows.shape[0], model_width)
        return (d_keys_part, d_values_part)

    d_keys_part, d_values_part = jax.vmap(per_sequence)(
        q_piece, d_piece, keys_own, values_own, lse_rows, delta_rows_all, lengths
    )
    d_mixed = jnp.concatenate([d_query_all, d_keys_part, d_values_part], axis=-1)
    rim_terms = jnp.stack(
        [taps[2] * d_mixed[:, 0], taps[1] * d_mixed[:, 0] + taps[2] * d_mixed[:, 1]], axis=1
    )
    back_rows = from_behind(rim_terms.astype(jnp.bfloat16), "seq", -1).astype(rim_terms.dtype)
    padded = jnp.concatenate(
        [d_mixed, jnp.zeros((seq_count, 2, 3 * model_width), jnp.float32)], axis=1
    )
    d_proj = (
        taps[0] * padded[:, :block_len]
        + taps[1] * padded[:, 1 : block_len + 1]
        + taps[2] * padded[:, 2:]
    )
    d_proj = d_proj + jnp.pad(back_rows, ((0, 0), (block_len - 2, 0), (0, 0)))
    d_proj_low = d_proj.astype(jnp.bfloat16)
    grad_taps = jnp.stack(
        [
            jnp.sum(d_mixed * extended[:, 2:], axis=(0, 1)),
            jnp.sum(d_mixed * extended[:, 1 : block_len + 1], axis=(0, 1)),
            jnp.sum(d_mixed * extended[:, :block_len], axis=(0, 1)),
        ]
    )
    grad_qkv = jnp.einsum(
        "scd,scn->dn", normed1_low, d_proj_low, preferred_element_type=jnp.float32
    )
    d_normed1 = jnp.einsum("scn,dn->scd", d_proj_low, w_qkv, preferred_element_type=jnp.float32)
    d_input_norm, grad_norm1 = norm_backward(resid, factor_one, gain_one, d_normed1)
    grad_input = d_hidden1 + d_input_norm
    shares = (
        lax.psum_scatter(
            grad_norm1.astype(jnp.bfloat16), "batch", scatter_dimension=0, tiled=True
        ).astype(jnp.float32),
        lax.psum_scatter(
            grad_qkv.astype(jnp.bfloat16), "batch", scatter_dimension=0, tiled=True
        ).astype(jnp.float32),
        lax.psum_scatter(
            grad_wout.astype(jnp.bfloat16), "batch", scatter_dimension=0, tiled=True
        ).astype(jnp.float32),
        lax.psum_scatter(
            grad_norm2.astype(jnp.bfloat16), "batch", scatter_dimension=0, tiled=True
        ).astype(jnp.float32),
        lax.psum_scatter(
            grad_up.astype(jnp.bfloat16), "batch", scatter_dimension=0, tiled=True
        ).astype(jnp.float32),
        lax.psum_scatter(
            grad_down.astype(jnp.bfloat16), "batch", scatter_dimension=0, tiled=True
        ).astype(jnp.float32),
    )
    totals = (
        lax.psum(shares[0].astype(jnp.bfloat16), "seq").astype(jnp.float32),
        lax.psum(shares[1].astype(jnp.bfloat16), "seq").astype(jnp.float32),
        lax.psum(shares[2].astype(jnp.bfloat16), "seq").astype(jnp.float32),
        lax.psum(shares[3].astype(jnp.bfloat16), "seq").astype(jnp.float32),
        lax.psum(shares[4].astype(jnp.bfloat16), "seq").astype(jnp.float32),
        lax.psum(shares[5].astype(jnp.bfloat16), "seq").astype(jnp.float32),
    )
    small = lax.psum((grad_taps, local_stats), ("seq", "batch"))
    block_rms = jnp.sqrt(small[1][:3] / (model_width * small[1][3]))
    return (
        stream_out,
        grad_input,
        totals[0],
        totals[1],
        small[0],
        totals[2],
        totals[3],
        totals[4],
        totals[5],
        block_rms,
    )


def solution(mesh):
    return jax.shard_map(
        shards,
        mesh=mesh,
        in_specs=(
            P("batch", "seq", None),
            P("batch"),
            P("batch", "seq"),
            P(),
            P(),
            P(),
            P(),
            P(),
            P(),
            P(),
            P("batch", "seq", None),
        ),
        out_specs=(
            P("batch", "seq", None),
            P("batch", "seq", None),
            P("batch"),
            P("batch", None),
            P(),
            P("batch", None),
            P("batch"),
            P("batch", None),
            P("batch", None),
            P(),
        ),
        check_vma=False,
    )
```

profile of v0, /device:TPU:0, one launch (start us, length us, event | category | flops | bytes accessed | tf_op | source)
XLA Modules:
  0.0 1237.5 jit_solution(3690341579583954142)
XLA Ops:
  37.0 17.5 %add_convert_fusion.1 = bf16[4,256,2304]{2,0,1:T(4,128)(2,1)S(1)} fusion(f32[4,258,2304]{2,0,1:T(4,128)} %constant_dynamic-update-slice_fusion.1, f32[2304]{0:T(1024)S(1)} %get-tuple-element.212, f32[2304]{0:T(1024)} %get-tuple-element.213, f32[2304]{0:T(1024)} %get-tuple-element.211, f32[4,256,2304]{2,1,0:T(8,128)} %copy-done.2), kind=kLoop, calls=%fused_computation.52 | loop fusion | flops 14155776 | bytes 33057792 | tf_op jit(solution)/shard_map/convert_element_type | solution.py:120
  64.8 70.0 %all-gather.7.cloned.1.call-done = bf16[4,2048,768]{2,0,1:T(4,128)(2,1)} async-done(((bf16[4,256,768]{2,0,1:T(4,128)(2,1)}), bf16[4,2048,768]{2,0,1:T(4,128)(2,1)}) %all-gather.7.cloned.1.call-update) | async-done | bytes 12582928 | tf_op jit(solution)/shard_map/all_gather | solution.py:125
  134.8 20.3 %copy.104 = bf16[4,2048,768]{1,2,0:T(8,128)(2,1)} copy(bf16[4,2048,768]{2,0,1:T(4,128)(2,1)} %all-gather.7.cloned.1.call-done) | data formatting | bytes 25165824 | tf_op jit(solution)/shard_map/while | solution.py:132
  155.1 53.8 %all-gather.5.cloned.1.call-done = bf16[4,2048,768]{2,0,1:T(4,128)(2,1)} async-done(((bf16[4,256,768]{2,0,1:T(4,128)(2,1)}), bf16[4,2048,768]{2,0,1:T(4,128)(2,1)}) %all-gather.5.cloned.1.call-update) | async-done | bytes 12582928 | tf_op jit(solution)/shard_map/all_gather | solution.py:126
  208.9 20.3 %copy.102 = bf16[4,2048,768]{1,2,0:T(8,128)(2,1)} copy(bf16[4,2048,768]{2,0,1:T(4,128)(2,1)} %all-gather.5.cloned.1.call-done) | data formatting | bytes 25165824 | tf_op jit(solution)/shard_map/while | solution.py:132
  229.8 170.0 %while.24 = (s32[]{:T(128)}, bf16[4,256,768]{1,2,0:T(8,128)(2,1)}, f32[4,12,256]{2,1,0:T(8,128)}, bf16[4,2048,768]{1,2,0:T(8,128)(2,1)}, s32[]{:T(128)}, /*index...) while((s32[]{:T(128)}, bf16[4,256,768]{1,2,0:T(8,128)(2,1)}, ...), condition=%wide.region_4.5_spmd, body=%wide.region_1.4_spmd.sunk | while | flops 1687158016 | bytes 98936960 | solution.py:132
  474.8 350.4 %while.25 = (s32[]{:T(128)}, f32[4,256,768]{2,0,1:T(4,128)}, f32[4,12,256]{2,1,0:T(8,128)}, bf16[4,2048,768]{1,2,0:T(8,128)(2,1)}, s32[]{:T(128)}, /*index=5*/s3...) while((s32[]{:T(128)}, f32[4,256,768]{2,0,1:T(4,128)}, ...), condition=%wide.region_9.10_spmd, body=%wide.region_7.9_spmd.sunk | while | flops 2486369536 | bytes 169195712 | solution.py:175
  502.7 19.8 %multiply_reduce_fusion.14 = (f32[12,256]{1,0:T(8,128)}, f32[12,256,2048]{2,1,0:T(8,128)}) fusion(f32[12,256,2048]{2,1,0:T(8,128)} %fusion.116, f32[12,256]{1,0:T(8,128)S(1)} %dynamic-slice_bitcast_fusion.2, pred[256,2048]{1,0:T(8,128)(4,1)} %fusion.117, bf16[256,12,64]{0,2,1:T(8,128)(2,1)} %bitcast.149, bf16[2048,12,64]{0,2,1:T(8,128)(2,1)} %bitcast.142), kind=kOutput, calls=%fused_computation.18.clone.1 | convolution fusion | flops 836760576 | bytes 54419456 | tf_op jit(solution)/shard_map/while/body/eval_jaxpr/qhe,khe->hqk/dot_general | solution.py:71
  522.5 20.4 %fusion.118 = f32[12,64,256]{2,1,0:T(8,128)} fusion(bf16[2048,12,64]{0,2,1:T(8,128)(2,1)} %bitcast.140, f32[12,256,2048]{2,1,0:T(8,128)} %get-tuple-element.413, f32[12,256,2048]{2,1,0:T(8,128)} %fusion.116, f32[12,256]{1,0:T(8,128)} %get-tuple-element.414, f32[12,256]{1,0:T(8,128)S(1)} %dynamic-slice_bitcast_fusion.2, pred[256,2048]{1,0:T(8,128)(4,1)} %fusion.117), kind=kOutput, calls=%fused_computation.24.clone.1 | convolution fusion | flops 843251712 | bytes 54812672 | tf_op jit(solution)/shard_map/while/body/eval_jaxpr/hqk,khe->qhe/dot_general | solution.py:78
  547.3 15.6 %dynamic_update_slice.24 = f32[4,256,768]{2,0,1:T(4,128)} dynamic-update-slice(f32[4,256,768]{2,0,1:T(4,128)} %get-tuple-element.455, f32[1,256,768]{2,0,1:T(1,128)} %copy.160, s32[]{:T(128)S(6)} %copy.178, s32[]{:T(128)} %constant.66.clone.1..sunk, s32[]{:T(128)} %constant.66.clone.1..sunk) | dynamic-update-slice | bytes 1572868 | tf_op jit(solution)/shard_map/while/body/jit(dynamic_update_index_in_dim)/dynamic_update_slice | solution.py:132
  590.6 19.8 %multiply_reduce_fusion.14 = (f32[12,256]{1,0:T(8,128)}, f32[12,256,2048]{2,1,0:T(8,128)}) fusion(f32[12,256,2048]{2,1,0:T(8,128)} %fusion.116, f32[12,256]{1,0:T(8,128)S(1)} %dynamic-slice_bitcast_fusion.2, pred[256,2048]{1,0:T(8,128)(4,1)} %fusion.117, bf16[256,12,64]{0,2,1:T(8,128)(2,1)} %bitcast.149, bf16[2048,12,64]{0,2,1:T(8,128)(2,1)} %bitcast.142), kind=kOutput, calls=%fused_computation.18.clone.1 | convolution fusion | flops 836760576 | bytes 54419456 | tf_op jit(solution)/shard_map/while/body/eval_jaxpr/qhe,khe->hqk/dot_general | solution.py:71
  610.4 20.3 %fusion.118 = f32[12,64,256]{2,1,0:T(8,128)} fusion(bf16[2048,12,64]{0,2,1:T(8,128)(2,1)} %bitcast.140, f32[12,256,2048]{2,1,0:T(8,128)} %get-tuple-element.413, f32[12,256,2048]{2,1,0:T(8,128)} %fusion.116, f32[12,256]{1,0:T(8,128)} %get-tuple-element.414, f32[12,256]{1,0:T(8,128)S(1)} %dynamic-slice_bitcast_fusion.2, pred[256,2048]{1,0:T(8,128)(4,1)} %fusion.117), kind=kOutput, calls=%fused_computation.24.clone.1 | convolution fusion | flops 843251712 | bytes 54812672 | tf_op jit(solution)/shard_map/while/body/eval_jaxpr/hqk,khe->qhe/dot_general | solution.py:78
  678.2 19.8 %multiply_reduce_fusion.14 = (f32[12,256]{1,0:T(8,128)}, f32[12,256,2048]{2,1,0:T(8,128)}) fusion(f32[12,256,2048]{2,1,0:T(8,128)} %fusion.116, f32[12,256]{1,0:T(8,128)S(1)} %dynamic-slice_bitcast_fusion.2, pred[256,2048]{1,0:T(8,128)(4,1)} %fusion.117, bf16[256,12,64]{0,2,1:T(8,128)(2,1)} %bitcast.149, bf16[2048,12,64]{0,2,1:T(8,128)(2,1)} %bitcast.142), kind=kOutput, calls=%fused_computation.18.clone.1 | convolution fusion | flops 836760576 | bytes 54419456 | tf_op jit(solution)/shard_map/while/body/eval_jaxpr/qhe,khe->hqk/dot_general | solution.py:71
  697.9 20.1 %fusion.118 = f32[12,64,256]{2,1,0:T(8,128)} fusion(bf16[2048,12,64]{0,2,1:T(8,128)(2,1)} %bitcast.140, f32[12,256,2048]{2,1,0:T(8,128)} %get-tuple-element.413, f32[12,256,2048]{2,1,0:T(8,128)} %fusion.116, f32[12,256]{1,0:T(8,128)} %get-tuple-element.414, f32[12,256]{1,0:T(8,128)S(1)} %dynamic-slice_bitcast_fusion.2, pred[256,2048]{1,0:T(8,128)(4,1)} %fusion.117), kind=kOutput, calls=%fused_computation.24.clone.1 | convolution fusion | flops 843251712 | bytes 54812672 | tf_op jit(solution)/shard_map/while/body/eval_jaxpr/hqk,khe->qhe/dot_general | solution.py:78
  765.5 19.8 %multiply_reduce_fusion.14 = (f32[12,256]{1,0:T(8,128)}, f32[12,256,2048]{2,1,0:T(8,128)}) fusion(f32[12,256,2048]{2,1,0:T(8,128)} %fusion.116, f32[12,256]{1,0:T(8,128)S(1)} %dynamic-slice_bitcast_fusion.2, pred[256,2048]{1,0:T(8,128)(4,1)} %fusion.117, bf16[256,12,64]{0,2,1:T(8,128)(2,1)} %bitcast.149, bf16[2048,12,64]{0,2,1:T(8,128)(2,1)} %bitcast.142), kind=kOutput, calls=%fused_computation.18.clone.1 | convolution fusion | flops 836760576 | bytes 54419456 | tf_op jit(solution)/shard_map/while/body/eval_jaxpr/qhe,khe->hqk/dot_general | solution.py:71
  785.2 20.1 %fusion.118 = f32[12,64,256]{2,1,0:T(8,128)} fusion(bf16[2048,12,64]{0,2,1:T(8,128)(2,1)} %bitcast.140, f32[12,256,2048]{2,1,0:T(8,128)} %get-tuple-element.413, f32[12,256,2048]{2,1,0:T(8,128)} %fusion.116, f32[12,256]{1,0:T(8,128)} %get-tuple-element.414, f32[12,256]{1,0:T(8,128)S(1)} %dynamic-slice_bitcast_fusion.2, pred[256,2048]{1,0:T(8,128)(4,1)} %fusion.117), kind=kOutput, calls=%fused_computation.24.clone.1 | convolution fusion | flops 843251712 | bytes 54812672 | tf_op jit(solution)/shard_map/while/body/eval_jaxpr/hqk,khe->qhe/dot_general | solution.py:78
  857.3 20.1 %copy.110 = bf16[4,2048,768]{1,2,0:T(8,128)(2,1)} copy(bf16[4,2048,768]{2,0,1:T(4,128)(2,1)} %all-gather.9.cloned.1.call-done) | data formatting | bytes 25165824 | tf_op jit(solution)/shard_map/all_gather | solution.py:183
  877.5 39.7 %fusion.62 = f32[4,12,2048,256]{3,2,1,0:T(8,128)} fusion(bf16[4,2048,12,64]{1,3,2,0:T(8,128)(2,1)} %bitcast.147, bf16[4,256,12,64]{1,3,2,0:T(8,128)(2,1)} %bitcast.153), kind=kOutput, calls=%fused_computation.137 | convolution fusion | flops 3221225472 | bytes 114819072 | tf_op jit(solution)/shard_map/vmap(qhe,khe->hqk)/dot_general | solution.py:41
  917.2 16.0 %copy.112 = bf16[4,2048,768]{1,2,0:T(8,128)(2,1)} copy(bf16[4,2048,768]{2,1,0:T(8,128)(2,1)} %all-gather.11.cloned.1.call-done) | data formatting | bytes 25165824 | tf_op jit(solution)/shard_map/all_gather | solution.py:184
  933.2 38.9 %fusion.13 = f32[4,12,64,256]{3,2,1,0:T(8,128)} fusion(bf16[4,2048,12,64]{1,3,2,0:T(8,128)(2,1)} %bitcast.150, f32[4,12,2048,256]{3,2,1,0:T(8,128)} %fusion.62, f32[4,12,2048]{2,1,0:T(8,128)} %all_gather.21, pred[4,2048,256]{2,1,0:T(8,128)(4,1)} %broadcast_and_fusion), kind=kOutput, calls=%fused_computation.38 | convolution fusion | flops 3321888768 | bytes 118882304 | tf_op jit(solution)/shard_map/vmap(hqk,qhe->khe)/dot_general | solution.py:202
  977.1 51.0 %fusion.42 = f32[4,12,64,256]{3,2,1,0:T(8,128)} fusion(bf16[4,2048,12,64]{1,3,2,0:T(8,128)(2,1)} %bitcast.148, f32[4,12,2048,256]{3,2,1,0:T(8,128)} %fusion.62, f32[4,12,2048]{2,1,0:T(8,128)} %all_gather.23, f32[4,12,2048]{2,1,0:T(8,128)} %all_gather.21, pred[4,2048,256]{2,1,0:T(8,128)(4,1)} %broadcast_and_fusion, bf16[4,2048,12,64]{1,3,2,0:T(8,128)(2,1)} %bitcast.151, ...), kind=kOutput, calls=%fused_computation.94 | convolution fusion | flops 6594232320 | bytes 133431296 | tf_op jit(solution)/shard_map/vmap(hqk,qhe->khe)/dot_general | solution.py:197
  1033.0 20.5 %multiply_reduce_fusion.2 = (f32[2304]{0:T(1024)}, f32[2304]{0:T(1024)}, f32[2304]{0:T(1024)S(1)}, f32[4,256,2304]{2,0,1:T(4,128)S(1)}) fusion(f32[4,258,2304]{2,0,1:T(4,128)} %constant_dynamic-update-slice_fusion.1, f32[4,256,768]{2,0,1:T(4,128)} %copy.116, f32[4,256,768]{2,0,1:T(4,128)} %copy.115, f32[4,256,768]{2,0,1:T(4,128)} %get-tuple-element.108, ...), kind=kLoop, calls=%fused_computation.49 | loop fusion | flops 18867456 | bytes 47213568 | tf_op jit(solution)/shard_map/reduce_sum | solution.py:231
  1082.8 47.2 %all-reduce.4 = (f32[3,2304]{1,0:T(4,128)}, f32[4]{0:T(128)S(1)}) all-reduce(f32[3,2304]{1,0:T(4,128)} %pad_maximum_fusion.2, f32[4]{0:T(128)} %pad_maximum_fusion.3), channel_id=1, replica_groups=mesh['seq'=8,'batch'=4] {'seq','batch'}, use_global_device_ids=true, to_apply=%region_19.20 | all-reduce | flops 6916 | bytes 55328 | tf_op jit(solution)/shard_map/psum | solution.py:269
  1188.3 34.7 %all-reduce.10.cloned.1.call-done = (bf16[192,2304]{1,0:T(8,128)(2,1)}, bf16[192,768]{1,0:T(8,128)(2,1)}, bf16[192,3072]{1,0:T(8,128)(2,1)}, bf16[768,768]{1,0:T(8,128)(2,1)}) async-done(((bf16[192,2304]{1,0:T(8,128)(2,1)}, bf16[192,768]{1,0:T(8,128)(2,1)}, bf16[192,3072]{1,0:T(8,128)(2,1)}, bf16[768,768]{1,0:T(8,128)(2,1)}), (bf16[192,2304]{1,0:T(8,128)(2,1)}, bf16[192,768]{1,0:T(8,128)(2,1)}, ...) | async-done | bytes 3538960 | tf_op jit(solution)/shard_map/psum | solution.py:263
  (267 shorter events, 595.7 us)
Async XLA Ops:
  7.2 127.6 %all-gather.7.cloned.1.call-start = ((), (), s32[]{:S(2)}) async-start(), calls=%async_computation.5 | async-start | bytes 14155776 | tf_op jit(solution)/shard_map/all_gather | solution.py:125
  19.7 3.3 collective-permute-start
  22.9 14.0 %copy-start.10 = (f32[2304]{0:T(1024)}, f32[2304]{0:T(1024)S(1)}, u32[]{:S(2)}) copy-start(f32[2304]{0:T(1024)S(1)} %get-tuple-element.212) | copy-start | bytes 27652
  57.4 151.4 %all-gather.5.cloned.1.call-start = ((), (), s32[]{:S(2)}) async-start(), calls=%async_computation.4 | async-start | bytes 14155776 | tf_op jit(solution)/shard_map/all_gather | solution.py:126
  58.2 799.2 %all-gather.9.cloned.1.call-start = ((), (), s32[]{:S(2)}) async-start(), calls=%async_computation.6 | async-start | bytes 14155776 | tf_op jit(solution)/shard_map/all_gather | solution.py:183
  64.5 852.7 %all-gather.11.cloned.1.call-start = ((), (), s32[]{:S(2)}) async-start(), calls=%async_computation.7 | async-start | bytes 14155776 | tf_op jit(solution)/shard_map/all_gather | solution.py:184
  399.8 13.6 %slice-start = ((s8[4718592]{0:T(1024)(128)(4,1)}), s8[4194304]{0:T(1024)(128)(4,1)S(1)}, s32[]{:S(2)}) async-start(s8[4718592]{0:T(1024)(128)(4,1)} %bitcast.157), calls=%async_computation.13 | async-start | bytes 8388608
  404.9 36.1 %copy-start.6 = (f32[4,256,768]{2,1,0:T(8,128)}, f32[4,256,768]{2,1,0:T(8,128)S(1)}, u32[]{:S(2)}) copy-start(f32[4,256,768]{2,1,0:T(8,128)S(1)} %get-tuple-element.267) | copy-start | bytes 9437188
  404.9 36.1 %copy-start.17 = (f32[4,256]{1,0:T(4,128)}, f32[4,256]{1,0:T(4,128)S(1)}, u32[]{:S(2)}) copy-start(f32[4,256]{1,0:T(4,128)S(1)} %get-tuple-element.287) | copy-start | bytes 12292
  446.4 684.8 %reduce-scatter.7.cloned.1.call-start = ((), (), s32[]{:S(2)}) async-start(), calls=%async_computation.9 | async-start | bytes 1474560 | tf_op jit(solution)/shard_map/reduce_scatter | solution.py:248
  452.5 678.8 %reduce-scatter.11.cloned.1.call-start = ((), (), s32[]{:S(2)}) async-start(), calls=%async_computation.11 | async-start | bytes 5898240 | tf_op jit(solution)/shard_map/reduce_scatter | solution.py:257
  474.1 657.1 %reduce-scatter.9.cloned.1.call-start = ((), (), s32[]{:S(2)}) async-start(), calls=%async_computation.10 | async-start | bytes 5898240 | tf_op jit(solution)/shard_map/reduce_scatter | solution.py:254
  857.3 287.2 %reduce-scatter.5.cloned.1.call-start = ((), (), s32[]{:S(2)}) async-start(), calls=%async_computation.8 | async-start | bytes 4423680 | tf_op jit(solution)/shard_map/reduce_scatter | solution.py:245
  1033.0 20.5 %copy-start.11 = (f32[2304]{0:T(1024)S(1)}, f32[2304]{0:T(1024)}, u32[]{:S(2)}) copy-start(f32[2304]{0:T(1024)} %copy-done.10) | copy-start | bytes 27652
  1033.0 20.5 %copy-start.12 = (f32[2304]{0:T(1024)S(1)}, f32[2304]{0:T(1024)}, u32[]{:S(2)}) copy-start(f32[2304]{0:T(1024)} %get-tuple-element.213) | copy-start | bytes 27652
  1033.0 24.4 %copy-start.13 = (f32[2304]{0:T(1024)S(1)}, f32[2304]{0:T(1024)}, u32[]{:S(2)}) copy-start(f32[2304]{0:T(1024)} %get-tuple-element.211) | copy-start | bytes 27652
  1053.6 15.0 %copy-start.4 = (bf16[4,256,768]{2,1,0:T(8,128)(2,1)S(1)}, bf16[4,256,768]{2,1,0:T(8,128)(2,1)}, u32[]{:S(2)}) copy-start(bf16[4,256,768]{2,1,0:T(8,128)(2,1)} %param.15) | copy-start | bytes 4718596
  1053.6 15.0 %copy-start.21 = (f32[4,256]{1,0:T(4,128)S(1)}, f32[4,256]{1,0:T(4,128)}, u32[]{:S(2)}) copy-start(f32[4,256]{1,0:T(4,128)} %copy-done.20) | copy-start | bytes 12292
  1053.6 15.0 %copy-start.24 = (f32[768]{0:T(1024)S(1)}, f32[768]{0:T(1024)}, u32[]{:S(2)}) copy-start(f32[768]{0:T(1024)} %copy-done.23) | copy-start | bytes 9220
  1053.7 3.8 collective-permute-start.1
  1074.2 148.8 %all-reduce.10.cloned.1.call-start = ((), (), s32[]{:S(2)}) async-start(), calls=%async_computation.12 | async-start | bytes 7077888 | tf_op jit(solution)/shard_map/psum | solution.py:263
  1077.5 67.5 %copy-start.22 = (f32[4,256]{1,0:T(4,128)S(1)}, f32[4,256]{1,0:T(4,128)}, u32[]{:S(2)}) copy-start(f32[4,256]{1,0:T(4,128)} %copy-done.20) | copy-start | bytes 12292
  1082.1 62.9 %copy-start.25 = (f32[768]{0:T(1024)S(1)}, f32[768]{0:T(1024)}, u32[]{:S(2)}) copy-start(f32[768]{0:T(1024)} %copy-done.23) | copy-start | bytes 9220
  1145.0 38.4 %copy-start.19 = (f32[4,256]{1,0:T(4,128)S(1)}, f32[4,256]{1,0:T(4,128)}, u32[]{:S(2)}) copy-start(f32[4,256]{1,0:T(4,128)} %get-tuple-element.284) | copy-start | bytes 12292
  (26 other events, 120.0 us)
Sparse Core Ops, SparseCore 0:
  57.5 77.2 all-gather.6
  136.7 72.1 all-gather.4
  210.8 72.1 all-gather.8
  446.5 72.1 all-gather.10
  520.9 29.1 reduce-scatter.6
  552.3 83.9 reduce-scatter.10
  857.4 85.4 reduce-scatter.8
  1074.3 70.0 reduce-scatter.4
  1148.1 74.8 all-reduce.9
where the time goes:
time: 1250 us; the launch traced here: 1240 us
  matrix products  510 us (41%)
  local copies, waits for them, and re-layouts  291 us (23%)
  waiting for transfers between devices  175 us (14%)
  other arithmetic  147 us (12%)
  blocking collectives  93.4 us (7%)
  between operations  15.8 us (1%)
    dot_general x9, matrix products, score_block(): jnp.einsum('qhe,khe->hqk', split_heads(q_rows), split_heads(k_rows), pref...  124 us
    dynamic_update_slice x16, local copies, waits for them, and re-layouts, shards(): lax.map(forward_one, (query, keys_all, values_all, lengths))  82.7 us
    dot_general x4, matrix products, attend_backward(): jnp.einsum('hqk,khe->qhe', d_scores, split_heads(k_rows), preferred_eleme...  81 us
    dot_general x4, matrix products, attend_backward(): jnp.einsum('qhe,khe->hqk', split_heads(d_rows), split_heads(v_rows), pref...  79.1 us
    all_gather x1, waiting for transfers between devices, shards(): lax.all_gather(keys_own, 'seq', axis=1, tiled=True)  70 us
    dynamic_slice x32, local copies, waits for them, and re-layouts, shards(): lax.map(forward_one, (query, keys_all, values_all, lengths))  68.3 us
    all_gather x1, waiting for transfers between devices, shards(): lax.all_gather(values_own, 'seq', axis=1, tiled=True)  53.8 us
    dot_general x1, matrix products, per_sequence(): jnp.einsum('hqk,qhe->khe', d_scores, split_heads(q_rows), preferred_eleme...  51 us
  transfers between devices with their start and end apart: 11, of which 5 were waited for; matrix products, arithmetic and copies ran while one was open for 71% of the time, Pallas kernels for 0%

commit v1 on v0

--- a/solution.py
+++ b/solution.py
@@ -260,7 +260,7 @@
     )
     totals = (
         lax.psum(shares[0].astype(jnp.bfloat16), "seq").astype(jnp.float32),
-        lax.psum(shares[1].astype(jnp.bfloat16), "seq").astype(jnp.float32),
+        jnp.sum(lax.all_gather(shares[1].astype(jnp.bfloat16), "seq"), axis=0).astype(jnp.float32),
         lax.psum(shares[2].astype(jnp.bfloat16), "seq").astype(jnp.float32),
         lax.psum(shares[3].astype(jnp.bfloat16), "seq").astype(jnp.float32),
         lax.psum(shares[4].astype(jnp.bfloat16), "seq").astype(jnp.float32),

time: 1250 us -> 1330 us (1.064)
  waiting for transfers between devices: 175 us -> 259 us
    reduce_scatter x1, waiting for transfers between devices: 13.2 us -> 68.8 us  [shards(): lax.psum_scatter(grad_qkv.astype(jnp.bfloat16), 'batch', scatter_dimensio...]
    psum x1, waiting for transfers between devices: 34.7 us -> 63.3 us  [shards(): lax.psum(shares[2].astype(jnp.bfloat16), 'seq').astype(jnp.float32)]
  transfers between devices with their start and end apart: 11 -> 12, of which waited for: 5 -> 5; matrix products, arithmetic and copies ran while one was open for 71% -> 67% of each run, Pallas kernels for 0% -> 0%
where the time goes in v1:
time: 1330 us; the launch traced here: 1320 us
  matrix products  511 us (38%)
  local copies, waits for them, and re-layouts  290 us (22%)
  waiting for transfers between devices  259 us (19%)
  other arithmetic  153 us (12%)
  blocking collectives  86.6 us (7%)
  between operations  16.1 us (1%)
    dot_general x9, matrix products, score_block(): jnp.einsum('qhe,khe->hqk', split_heads(q_rows), split_heads(k_rows), pref...  124 us
    dynamic_update_slice x16, local copies, waits for them, and re-layouts, shards(): lax.map(forward_one, (query, keys_all, values_all, lengths))  82.7 us
    dot_general x4, matrix products, attend_backward(): jnp.einsum('hqk,khe->qhe', d_scores, split_heads(k_rows), preferred_eleme...  81 us
    dot_general x4, matrix products, attend_backward(): jnp.einsum('qhe,khe->hqk', split_heads(d_rows), split_heads(v_rows), pref...  79.2 us
    all_gather x1, waiting for transfers between devices, shards(): lax.all_gather(keys_own, 'seq', axis=1, tiled=True)  70 us
    reduce_scatter x1, waiting for transfers between devices, shards(): lax.psum_scatter(grad_qkv.astype(jnp.bfloat16), 'batch', scatter_dimensio...  68.8 us
    dynamic_slice x32, local copies, waits for them, and re-layouts, shards(): lax.map(forward_one, (query, keys_all, values_all, lengths))  68.2 us
    psum x1, waiting for transfers between devices, shards(): lax.psum(shares[2].astype(jnp.bfloat16), 'seq').astype(jnp.float32)  63.3 us
  transfers between devices with their start and end apart: 12, of which 5 were waited for; matrix products, arithmetic and copies ran while one was open for 67% of the time, Pallas kernels for 0%

profile of v1, /device:TPU:0, one launch (start us, length us, event | category | flops | bytes accessed | tf_op | source)
XLA Modules:
  0.0 1321.5 jit_solution(17202872314901679159)
XLA Ops:
  37.0 17.5 %add_convert_fusion.1 = bf16[4,256,2304]{2,0,1:T(4,128)(2,1)S(1)} fusion(f32[4,258,2304]{2,0,1:T(4,128)} %constant_dynamic-update-slice_fusion.1, f32[2304]{0:T(1024)S(1)} %get-tuple-element.212, f32[2304]{0:T(1024)} %get-tuple-element.213, f32[2304]{0:T(1024)} %get-tuple-element.211, f32[4,256,2304]{2,1,0:T(8,128)} %copy-done.2), kind=kLoop, calls=%fused_computation.52 | loop fusion | flops 14155776 | bytes 33057792 | tf_op jit(solution)/shard_map/convert_element_type | solution.py:120
  64.8 70.0 %all-gather.9.cloned.1.call-done = bf16[4,2048,768]{2,0,1:T(4,128)(2,1)} async-done(((bf16[4,256,768]{2,0,1:T(4,128)(2,1)}), bf16[4,2048,768]{2,0,1:T(4,128)(2,1)}) %all-gather.9.cloned.1.call-update) | async-done | bytes 12582928 | tf_op jit(solution)/shard_map/all_gather | solution.py:125
  134.8 20.3 %copy.104 = bf16[4,2048,768]{1,2,0:T(8,128)(2,1)} copy(bf16[4,2048,768]{2,0,1:T(4,128)(2,1)} %all-gather.9.cloned.1.call-done) | data formatting | bytes 25165824 | tf_op jit(solution)/shard_map/while | solution.py:132
  155.1 53.7 %all-gather.7.cloned.1.call-done = bf16[4,2048,768]{2,0,1:T(4,128)(2,1)} async-done(((bf16[4,256,768]{2,0,1:T(4,128)(2,1)}), bf16[4,2048,768]{2,0,1:T(4,128)(2,1)}) %all-gather.7.cloned.1.call-update) | async-done | bytes 12582928 | tf_op jit(solution)/shard_map/all_gather | solution.py:126
  208.9 20.3 %copy.102 = bf16[4,2048,768]{1,2,0:T(8,128)(2,1)} copy(bf16[4,2048,768]{2,0,1:T(4,128)(2,1)} %all-gather.7.cloned.1.call-done) | data formatting | bytes 25165824 | tf_op jit(solution)/shard_map/while | solution.py:132
  229.7 170.4 %while.24 = (s32[]{:T(128)}, bf16[4,256,768]{1,2,0:T(8,128)(2,1)}, f32[4,12,256]{2,1,0:T(8,128)}, bf16[4,2048,768]{1,2,0:T(8,128)(2,1)}, s32[]{:T(128)}, /*index...) while((s32[]{:T(128)}, bf16[4,256,768]{1,2,0:T(8,128)(2,1)}, ...), condition=%wide.region_4.5_spmd, body=%wide.region_1.4_spmd.sunk | while | flops 1687158016 | bytes 98936960 | solution.py:132
  475.2 350.5 %while.25 = (s32[]{:T(128)}, f32[4,256,768]{2,0,1:T(4,128)}, f32[4,12,256]{2,1,0:T(8,128)}, bf16[4,2048,768]{1,2,0:T(8,128)(2,1)}, s32[]{:T(128)}, /*index=5*/s3...) while((s32[]{:T(128)}, f32[4,256,768]{2,0,1:T(4,128)}, ...), condition=%wide.region_9.10_spmd, body=%wide.region_7.9_spmd.sunk | while | flops 2486369536 | bytes 169195712 | solution.py:175
  503.1 19.8 %multiply_reduce_fusion.14 = (f32[12,256]{1,0:T(8,128)}, f32[12,256,2048]{2,1,0:T(8,128)}) fusion(f32[12,256,2048]{2,1,0:T(8,128)} %fusion.116, f32[12,256]{1,0:T(8,128)S(1)} %dynamic-slice_bitcast_fusion.2, pred[256,2048]{1,0:T(8,128)(4,1)} %fusion.117, bf16[256,12,64]{0,2,1:T(8,128)(2,1)} %bitcast.150, bf16[2048,12,64]{0,2,1:T(8,128)(2,1)} %bitcast.143), kind=kOutput, calls=%fused_computation.18.clone.1 | convolution fusion | flops 836760576 | bytes 54419456 | tf_op jit(solution)/shard_map/while/body/eval_jaxpr/qhe,khe->hqk/dot_general | solution.py:71
  522.9 20.4 %fusion.118 = f32[12,64,256]{2,1,0:T(8,128)} fusion(bf16[2048,12,64]{0,2,1:T(8,128)(2,1)} %bitcast.141, f32[12,256,2048]{2,1,0:T(8,128)} %get-tuple-element.412, f32[12,256,2048]{2,1,0:T(8,128)} %fusion.116, f32[12,256]{1,0:T(8,128)} %get-tuple-element.413, f32[12,256]{1,0:T(8,128)S(1)} %dynamic-slice_bitcast_fusion.2, pred[256,2048]{1,0:T(8,128)(4,1)} %fusion.117), kind=kOutput, calls=%fused_computation.24.clone.1 | convolution fusion | flops 843251712 | bytes 54812672 | tf_op jit(solution)/shard_map/while/body/eval_jaxpr/hqk,khe->qhe/dot_general | solution.py:78
  591.0 19.8 %multiply_reduce_fusion.14 = (f32[12,256]{1,0:T(8,128)}, f32[12,256,2048]{2,1,0:T(8,128)}) fusion(f32[12,256,2048]{2,1,0:T(8,128)} %fusion.116, f32[12,256]{1,0:T(8,128)S(1)} %dynamic-slice_bitcast_fusion.2, pred[256,2048]{1,0:T(8,128)(4,1)} %fusion.117, bf16[256,12,64]{0,2,1:T(8,128)(2,1)} %bitcast.150, bf16[2048,12,64]{0,2,1:T(8,128)(2,1)} %bitcast.143), kind=kOutput, calls=%fused_computation.18.clone.1 | convolution fusion | flops 836760576 | bytes 54419456 | tf_op jit(solution)/shard_map/while/body/eval_jaxpr/qhe,khe->hqk/dot_general | solution.py:71
  610.8 20.3 %fusion.118 = f32[12,64,256]{2,1,0:T(8,128)} fusion(bf16[2048,12,64]{0,2,1:T(8,128)(2,1)} %bitcast.141, f32[12,256,2048]{2,1,0:T(8,128)} %get-tuple-element.412, f32[12,256,2048]{2,1,0:T(8,128)} %fusion.116, f32[12,256]{1,0:T(8,128)} %get-tuple-element.413, f32[12,256]{1,0:T(8,128)S(1)} %dynamic-slice_bitcast_fusion.2, pred[256,2048]{1,0:T(8,128)(4,1)} %fusion.117), kind=kOutput, calls=%fused_computation.24.clone.1 | convolution fusion | flops 843251712 | bytes 54812672 | tf_op jit(solution)/shard_map/while/body/eval_jaxpr/hqk,khe->qhe/dot_general | solution.py:78
  678.5 19.8 %multiply_reduce_fusion.14 = (f32[12,256]{1,0:T(8,128)}, f32[12,256,2048]{2,1,0:T(8,128)}) fusion(f32[12,256,2048]{2,1,0:T(8,128)} %fusion.116, f32[12,256]{1,0:T(8,128)S(1)} %dynamic-slice_bitcast_fusion.2, pred[256,2048]{1,0:T(8,128)(4,1)} %fusion.117, bf16[256,12,64]{0,2,1:T(8,128)(2,1)} %bitcast.150, bf16[2048,12,64]{0,2,1:T(8,128)(2,1)} %bitcast.143), kind=kOutput, calls=%fused_computation.18.clone.1 | convolution fusion | flops 836760576 | bytes 54419456 | tf_op jit(solution)/shard_map/while/body/eval_jaxpr/qhe,khe->hqk/dot_general | solution.py:71
  698.3 20.1 %fusion.118 = f32[12,64,256]{2,1,0:T(8,128)} fusion(bf16[2048,12,64]{0,2,1:T(8,128)(2,1)} %bitcast.141, f32[12,256,2048]{2,1,0:T(8,128)} %get-tuple-element.412, f32[12,256,2048]{2,1,0:T(8,128)} %fusion.116, f32[12,256]{1,0:T(8,128)} %get-tuple-element.413, f32[12,256]{1,0:T(8,128)S(1)} %dynamic-slice_bitcast_fusion.2, pred[256,2048]{1,0:T(8,128)(4,1)} %fusion.117), kind=kOutput, calls=%fused_computation.24.clone.1 | convolution fusion | flops 843251712 | bytes 54812672 | tf_op jit(solution)/shard_map/while/body/eval_jaxpr/hqk,khe->qhe/dot_general | solution.py:78
  765.8 19.8 %multiply_reduce_fusion.14 = (f32[12,256]{1,0:T(8,128)}, f32[12,256,2048]{2,1,0:T(8,128)}) fusion(f32[12,256,2048]{2,1,0:T(8,128)} %fusion.116, f32[12,256]{1,0:T(8,128)S(1)} %dynamic-slice_bitcast_fusion.2, pred[256,2048]{1,0:T(8,128)(4,1)} %fusion.117, bf16[256,12,64]{0,2,1:T(8,128)(2,1)} %bitcast.150, bf16[2048,12,64]{0,2,1:T(8,128)(2,1)} %bitcast.143), kind=kOutput, calls=%fused_computation.18.clone.1 | convolution fusion | flops 836760576 | bytes 54419456 | tf_op jit(solution)/shard_map/while/body/eval_jaxpr/qhe,khe->hqk/dot_general | solution.py:71
  785.6 20.1 %fusion.118 = f32[12,64,256]{2,1,0:T(8,128)} fusion(bf16[2048,12,64]{0,2,1:T(8,128)(2,1)} %bitcast.141, f32[12,256,2048]{2,1,0:T(8,128)} %get-tuple-element.412, f32[12,256,2048]{2,1,0:T(8,128)} %fusion.116, f32[12,256]{1,0:T(8,128)} %get-tuple-element.413, f32[12,256]{1,0:T(8,128)S(1)} %dynamic-slice_bitcast_fusion.2, pred[256,2048]{1,0:T(8,128)(4,1)} %fusion.117), kind=kOutput, calls=%fused_computation.24.clone.1 | convolution fusion | flops 843251712 | bytes 54812672 | tf_op jit(solution)/shard_map/while/body/eval_jaxpr/hqk,khe->qhe/dot_general | solution.py:78
  857.8 20.1 %copy.110 = bf16[4,2048,768]{1,2,0:T(8,128)(2,1)} copy(bf16[4,2048,768]{2,0,1:T(4,128)(2,1)} %all-gather.11.cloned.1.call-done) | data formatting | bytes 25165824 | tf_op jit(solution)/shard_map/all_gather | solution.py:183
  877.9 39.7 %fusion.62 = f32[4,12,2048,256]{3,2,1,0:T(8,128)} fusion(bf16[4,2048,12,64]{1,3,2,0:T(8,128)(2,1)} %bitcast.148, bf16[4,256,12,64]{1,3,2,0:T(8,128)(2,1)} %bitcast.154), kind=kOutput, calls=%fused_computation.137 | convolution fusion | flops 3221225472 | bytes 114819072 | tf_op jit(solution)/shard_map/vmap(qhe,khe->hqk)/dot_general | solution.py:41
  917.6 16.7 %copy.112 = bf16[4,2048,768]{1,2,0:T(8,128)(2,1)} copy(bf16[4,2048,768]{2,1,0:T(8,128)(2,1)} %all-gather.13.cloned.1.call-done) | data formatting | bytes 25165824 | tf_op jit(solution)/shard_map/all_gather | solution.py:184
  934.3 38.9 %fusion.13 = f32[4,12,64,256]{3,2,1,0:T(8,128)} fusion(bf16[4,2048,12,64]{1,3,2,0:T(8,128)(2,1)} %bitcast.151, f32[4,12,2048,256]{3,2,1,0:T(8,128)} %fusion.62, f32[4,12,2048]{2,1,0:T(8,128)} %all_gather.27, pred[4,2048,256]{2,1,0:T(8,128)(4,1)} %broadcast_and_fusion), kind=kOutput, calls=%fused_computation.38 | convolution fusion | flops 3321888768 | bytes 118882304 | tf_op jit(solution)/shard_map/vmap(hqk,qhe->khe)/dot_general | solution.py:202
  978.2 51.0 %fusion.42 = f32[4,12,64,256]{3,2,1,0:T(8,128)} fusion(bf16[4,2048,12,64]{1,3,2,0:T(8,128)(2,1)} %bitcast.149, f32[4,12,2048,256]{3,2,1,0:T(8,128)} %fusion.62, f32[4,12,2048]{2,1,0:T(8,128)} %all_gather.29, f32[4,12,2048]{2,1,0:T(8,128)} %all_gather.27, pred[4,2048,256]{2,1,0:T(8,128)(4,1)} %broadcast_and_fusion, bf16[4,2048,12,64]{1,3,2,0:T(8,128)(2,1)} %bitcast.152, ...), kind=kOutput, calls=%fused_computation.94 | convolution fusion | flops 6594232320 | bytes 133431296 | tf_op jit(solution)/shard_map/vmap(hqk,qhe->khe)/dot_general | solution.py:197
  1034.2 20.5 %multiply_reduce_fusion.2 = (f32[2304]{0:T(1024)}, f32[2304]{0:T(1024)}, f32[2304]{0:T(1024)S(1)}, f32[4,256,2304]{2,0,1:T(4,128)S(1)}) fusion(f32[4,258,2304]{2,0,1:T(4,128)} %constant_dynamic-update-slice_fusion.1, f32[4,256,768]{2,0,1:T(4,128)} %copy.116, f32[4,256,768]{2,0,1:T(4,128)} %copy.115, f32[4,256,768]{2,0,1:T(4,128)} %get-tuple-element.108, ...), kind=kLoop, calls=%fused_computation.49 | loop fusion | flops 18867456 | bytes 47213568 | tf_op jit(solution)/shard_map/reduce_sum | solution.py:231
  1075.7 68.8 %reduce-scatter.5.cloned.1.call-done = bf16[192,2304]{1,0:T(8,128)(2,1)} async-done(((bf16[768,2304]{1,0:T(8,128)(2,1)}), bf16[192,2304]{1,0:T(8,128)(2,1)}) %reduce-scatter.5.cloned.1.call-update) | async-done | bytes 884752 | tf_op jit(solution)/shard_map/reduce_scatter | solution.py:245
  1150.9 63.3 %all-reduce.10.cloned.1.call-done = (bf16[192,768]{1,0:T(8,128)(2,1)}, bf16[192,3072]{1,0:T(8,128)(2,1)}, bf16[768,768]{1,0:T(8,128)(2,1)}) async-done(((bf16[192,768]{1,0:T(8,128)(2,1)}, bf16[192,3072]{1,0:T(8,128)(2,1)}, bf16[768,768]{1,0:T(8,128)(2,1)}), (bf16[192,768]{1,0:T(8,128)(2,1)}, bf16[192,3072]{1,0:T(8,128)(2,1)}, bf16[768,768]{1,0:T(8,128)(2,1)})) %all-reduce.10.cloned.1.call-update) | async-done | bytes 2654224 | tf_op jit(solution)/shard_map/psum | solution.py:264
  1221.4 40.7 %all-reduce.4 = (f32[3,2304]{1,0:T(4,128)}, f32[4]{0:T(128)S(1)}) all-reduce(f32[3,2304]{1,0:T(4,128)} %pad_maximum_fusion.2, f32[4]{0:T(128)} %pad_maximum_fusion.3), channel_id=1, replica_groups=mesh['seq'=8,'batch'=4] {'seq','batch'}, use_global_device_ids=true, to_apply=%region_19.20 | all-reduce | flops 6916 | bytes 55328 | tf_op jit(solution)/shard_map/psum | solution.py:269
  (273 shorter events, 603.4 us)
Async XLA Ops:
  7.2 127.6 %all-gather.9.cloned.1.call-start = ((), (), s32[]{:S(2)}) async-start(), calls=%async_computation.5 | async-start | bytes 14155776 | tf_op jit(solution)/shard_map/all_gather | solution.py:125
  19.7 3.3 collective-permute-start
  57.4 151.4 %all-gather.7.cloned.1.call-start = ((), (), s32[]{:S(2)}) async-start(), calls=%async_computation.4 | async-start | bytes 14155776 | tf_op jit(solution)/shard_map/all_gather | solution.py:126
  58.2 799.6 %all-gather.11.cloned.1.call-start = ((), (), s32[]{:S(2)}) async-start(), calls=%async_computation.6 | async-start | bytes 14155776 | tf_op jit(solution)/shard_map/all_gather | solution.py:183
  64.5 853.1 %all-gather.13.cloned.1.call-start = ((), (), s32[]{:S(2)}) async-start(), calls=%async_computation.7 | async-start | bytes 14155776 | tf_op jit(solution)/shard_map/all_gather | solution.py:184
  405.2 36.1 %copy-start.6 = (f32[4,256,768]{2,1,0:T(8,128)}, f32[4,256,768]{2,1,0:T(8,128)S(1)}, u32[]{:S(2)}) copy-start(f32[4,256,768]{2,1,0:T(8,128)S(1)} %get-tuple-element.266) | copy-start | bytes 9437188
  405.2 36.1 %copy-start.18 = (f32[4,256]{1,0:T(4,128)}, f32[4,256]{1,0:T(4,128)S(1)}, u32[]{:S(2)}) copy-start(f32[4,256]{1,0:T(4,128)S(1)} %get-tuple-element.286) | copy-start | bytes 12292
  446.8 628.2 %reduce-scatter.7.cloned.1.call-start = ((), (), s32[]{:S(2)}) async-start(), calls=%async_computation.9 | async-start | bytes 1474560 | tf_op jit(solution)/shard_map/reduce_scatter | solution.py:248
  452.8 622.2 %reduce-scatter.11.cloned.1.call-start = ((), (), s32[]{:S(2)}) async-start(), calls=%async_computation.11 | async-start | bytes 5898240 | tf_op jit(solution)/shard_map/reduce_scatter | solution.py:257
  474.5 600.5 %reduce-scatter.9.cloned.1.call-start = ((), (), s32[]{:S(2)}) async-start(), calls=%async_computation.10 | async-start | bytes 5898240 | tf_op jit(solution)/shard_map/reduce_scatter | solution.py:254
  857.7 286.8 %reduce-scatter.5.cloned.1.call-start = ((), (), s32[]{:S(2)}) async-start(), calls=%async_computation.8 | async-start | bytes 4423680 | tf_op jit(solution)/shard_map/reduce_scatter | solution.py:245
  1034.2 20.6 %copy-start.10 = (f32[2304]{0:T(1024)S(1)}, f32[2304]{0:T(1024)}, u32[]{:S(2)}) copy-start(f32[2304]{0:T(1024)} %copy-done.9) | copy-start | bytes 27652
  1034.2 20.6 %copy-start.11 = (f32[2304]{0:T(1024)S(1)}, f32[2304]{0:T(1024)}, u32[]{:S(2)}) copy-start(f32[2304]{0:T(1024)} %get-tuple-element.213) | copy-start | bytes 27652
  1034.2 23.9 %copy-start.12 = (f32[2304]{0:T(1024)S(1)}, f32[2304]{0:T(1024)}, u32[]{:S(2)}) copy-start(f32[2304]{0:T(1024)} %get-tuple-element.211) | copy-start | bytes 27652
  1054.8 14.5 %copy-start.4 = (bf16[4,256,768]{2,1,0:T(8,128)(2,1)S(1)}, bf16[4,256,768]{2,1,0:T(8,128)(2,1)}, u32[]{:S(2)}) copy-start(bf16[4,256,768]{2,1,0:T(8,128)(2,1)} %param.15) | copy-start | bytes 4718596
  1054.8 14.5 %copy-start.22 = (f32[4,256]{1,0:T(4,128)S(1)}, f32[4,256]{1,0:T(4,128)}, u32[]{:S(2)}) copy-start(f32[4,256]{1,0:T(4,128)} %copy-done.21) | copy-start | bytes 12292
  1054.8 14.5 %copy-start.25 = (f32[768]{0:T(1024)S(1)}, f32[768]{0:T(1024)}, u32[]{:S(2)}) copy-start(f32[768]{0:T(1024)} %copy-done.24) | copy-start | bytes 9220
  1054.8 3.2 collective-permute-start.1
  1074.9 71.6 %copy-start.16 = (f32[4,256]{1,0:T(4,128)S(1)}, f32[4,256]{1,0:T(4,128)}, u32[]{:S(2)}) copy-start(f32[4,256]{1,0:T(4,128)} %get-tuple-element.263) | copy-start | bytes 12292
  1074.9 139.3 %all-reduce.10.cloned.1.call-start = ((), (), s32[]{:S(2)}) async-start(), calls=%async_computation.13 | async-start | bytes 5308416 | tf_op jit(solution)/shard_map/psum | solution.py:264
  1075.6 231.2 %all-gather.15.cloned.1.call-start = ((), (), s32[]{:S(2)}) async-start(), calls=%async_computation.12 | async-start | bytes 7962624 | tf_op jit(solution)/shard_map/all_gather | solution.py:263
  1216.1 47.7 %copy-start.23 = (f32[4,256]{1,0:T(4,128)S(1)}, f32[4,256]{1,0:T(4,128)}, u32[]{:S(2)}) copy-start(f32[4,256]{1,0:T(4,128)} %copy-done.21) | copy-start | bytes 12292
  1263.8 38.1 %copy-start.20 = (f32[4,256]{1,0:T(4,128)S(1)}, f32[4,256]{1,0:T(4,128)}, u32[]{:S(2)}) copy-start(f32[4,256]{1,0:T(4,128)} %get-tuple-element.283) | copy-start | bytes 12292
  1263.8 38.1 %copy-start.26 = (f32[768]{0:T(1024)S(1)}, f32[768]{0:T(1024)}, u32[]{:S(2)}) copy-start(f32[768]{0:T(1024)} %copy-done.24) | copy-start | bytes 9220
  (28 other events, 149.3 us)
Sparse Core Ops, SparseCore 0:
  57.5 77.2 all-gather.8
  136.7 72.1 all-gather.6
  210.8 72.1 all-gather.10
  446.9 72.2 all-gather.12
  521.3 29.1 reduce-scatter.6
  552.7 83.9 reduce-scatter.10
  857.8 85.3 reduce-scatter.8
  1075.0 69.4 reduce-scatter.4
  1148.1 66.0 all-reduce.9
  1216.1 49.7 all-gather.14
